TPU v7x, 128 devices: a whole 4x4x4 slice. The times are simulated.
128 devices in a mesh: req: 8 (over z, core), tok: 16 (over y, x).
Axes of the slice: x: 4, y: 4, z: 4, core: 2. Of those that a mesh axis runs over, the one named last changes fastest.
Arguments:
- draft_ids: int32 [32, 16], replicated, may hold values from 0 to 65535
- lengths: int32 [32], replicated, may hold values from 1 to 16384, as said below
- current_slot: int32 [32], replicated, may hold values from 0 to 31, as said below
- new_slot: int32 [32], replicated, may hold values from 0 to 31, as said below
- accepted: int32 [32], replicated, may hold values from 1 to 16, as said below
- embed_table: bfloat16 [65536, 3072], P(('req', 'tok')), may hold values from -6.5 to 6.5
- mixer_gain: float32 [3072], replicated, may hold values from 0.5 to 1.5
- query_weight: bfloat16 [3072, 768], replicated, may hold values from -0.3049512 to 0.3049512
- keyvalue_weight: bfloat16 [3072, 256], replicated, may hold values from -0.109375 to 0.109375
- key_cache: bfloat16 [32, 16384, 128], P('req', 'tok'), may hold values from -6 to 6
- value_cache: bfloat16 [32, 16384, 128], P('req', 'tok'), may hold values from -6 to 6
- attention_out: bfloat16 [768, 3072], P(None, 'tok'), may hold values from -0.21875 to 0.21875
- mamba_input: bfloat16 [3072, 2048], P(None, 'tok'), may hold values from -0.109375 to 0.109375
- mamba_gate: bfloat16 [3072, 2048], P(None, 'tok'), may hold values from -0.109375 to 0.109375
- state_proj: bfloat16 [3072, 512], replicated, may hold values from -0.02734375 to 0.02734375
- mamba_step: bfloat16 [3072, 16], P(None, 'tok'), may hold values from -0.109375 to 0.109375
- step_bias: float32 [16], P('tok'), may hold values from -4 to 0
- decay_log: float32 [16], P('tok'), may hold values from -2 to 1.5
- skip_gain: float32 [16], P('tok'), may hold values from 0.5 to 1.5
- states: float32 [32, 16, 128, 256], P('req', 'tok'), may hold values from -1.5 to 1.5
- mamba_out: bfloat16 [2048, 3072], P('tok'), may hold values from -0.125 to 0.125
- mlp_gain: float32 [3072], replicated, may hold values from 0.5 to 1.5
- gate_weight: bfloat16 [3072, 12288], P(None, ('req', 'tok')), may hold values from -0.109375 to 0.109375
- up_weight: bfloat16 [3072, 12288], P(None, ('req', 'tok')), may hold values from -0.109375 to 0.109375
- down_weight: bfloat16 [3072, 12288], P(None, ('req', 'tok')), may hold values from -0.0546875 to 0.0546875
Outputs:
- hidden_out: bfloat16 [512, 3072], P(('req', 'tok'))
- new_states: float32 [32, 16, 128, 256], P('req', 'tok')
Inputs may be any that keep to these rules, and one draw needn't show every extreme that they name: `lengths`: some request has exactly 16384 cached positions and some exactly one. `current_slot`: a permutation: each slot holds one request. `new_slot`: a permutation: each slot receives one request. `accepted`: some request accepts all 16 drafts and some exactly one.
All inputs are finite; a program needn't handle non-finite values.
Results may differ from a plain program's by a relative error of at most 0.02.
Values may be sent and summed in bfloat16 or wider, within the bound.
No kernel may reach another device: no remote copies, remote signals or barrier semaphores. Data moves between devices by JAX's collectives and lax.ppermute only.
A program may use at most 128 MiB of HBM per device.

v0:
```python
import jax
import jax.numpy as jnp
from jax import lax
from jax.sharding import PartitionSpec as P


def rms_rows(table_rows, norm_gain):
    values = table_rows.astype(jnp.float32)
    factor = lax.rsqrt(jnp.mean(values * values, axis=-1, keepdims=True) + 1e-05)
    return (values * factor * norm_gain).astype(jnp.bfloat16)


def inverse_of(mapping):
    places = jnp.arange(mapping.shape[0], dtype=jnp.int32)
    matches = mapping[None, :] == places[:, None]
    return jnp.sum(jnp.where(matches, places[None, :], 0), axis=1)


def recurrence(start_states, decay_rate, inputs, state_in, state_read, accept_count):

    def advance(state_pair, step_items):
        current, chosen = state_pair
        step_decay, step_input, step_in, step_read, step_index = step_items
        current = (
            step_decay[:, :, None, None] * current
            + step_input[..., None] * step_in[:, None, None, :]
        )
        readout = jnp.sum(current * step_read[:, None, None, :], axis=-1)
        chosen = jnp.where((accept_count == step_index + 1)[:, None, None, None], current, chosen)
        return ((current, chosen), readout)

    sequence = (
        jnp.swapaxes(decay_rate, 0, 1),
        jnp.swapaxes(inputs, 0, 1),
        jnp.swapaxes(state_in, 0, 1),
        jnp.swapaxes(state_read, 0, 1),
        jnp.arange(decay_rate.shape[1], dtype=jnp.int32),
    )
    (current, chosen), readouts = lax.scan(advance, (start_states, start_states), sequence)
    return (jnp.swapaxes(readouts, 0, 1), chosen)


def feed_units(block_rows, gate_cols, up_cols, down_cols):
    gate_part = jnp.dot(block_rows, gate_cols, preferred_element_type=jnp.float32)
    up_part = jnp.dot(block_rows, up_cols, preferred_element_type=jnp.float32)
    hidden = (jax.nn.silu(gate_part) * up_part).astype(jnp.bfloat16)
    return lax.dot_general(
        hidden, down_cols, (((1,), (1,)), ((), ())), preferred_element_type=jnp.float32
    )


def local(
    draft_ids,
    lengths,
    current_slot,
    new_slot,
    accepted,
    embed_table,
    mixer_gain,
    query_weight,
    keyvalue_weight,
    key_cache,
    value_cache,
    attention_out,
    mamba_input,
    mamba_gate,
    state_proj,
    mamba_step,
    step_bias,
    decay_log,
    skip_gain,
    states,
    mamba_out,
    mlp_gain,
    gate_weight,
    up_weight,
    down_weight,
):
    members = lax.axis_size("tok")
    group_index = lax.axis_index("req")
    member = lax.axis_index("tok")
    slots_dev, cache_dev, head_size = key_cache.shape
    draft_len = draft_ids.shape[1]
    group_tokens = slots_dev * draft_len
    vocab_dev = embed_table.shape[0]
    query_heads = query_weight.shape[1] // head_size
    heads_dev = step_bias.shape[0]
    mamba_head = mamba_input.shape[1] // heads_dev
    state_size = state_proj.shape[1] // 2
    slot_owner = inverse_of(current_slot)
    token_ids = jnp.take(draft_ids, slot_owner, axis=0).reshape(-1)
    vocab_start = (group_index * members + member) * vocab_dev
    wanted = token_ids - vocab_start
    inside = (wanted >= 0) & (wanted < vocab_dev)
    picked = jnp.take(embed_table, jnp.clip(wanted, 0, vocab_dev - 1), axis=0)
    embedded = lax.psum_scatter(
        jnp.where(inside[:, None], picked.astype(jnp.float32), 0.0),
        ("req", "tok"),
        scatter_dimension=0,
        tiled=True,
    ).astype(jnp.bfloat16)
    normed = rms_rows(embedded, mixer_gain)
    gathered = lax.all_gather(normed, "tok", axis=0, tiled=True)
    queries = jnp.dot(gathered, query_weight, preferred_element_type=jnp.float32).astype(
        jnp.bfloat16
    )
    queries = queries.reshape(slots_dev, draft_len, query_heads, head_size)
    keyvalue = jnp.dot(gathered, keyvalue_weight, preferred_element_type=jnp.float32).astype(
        jnp.bfloat16
    )
    keyvalue = keyvalue.reshape(slots_dev, draft_len, 2, head_size)
    local_owner = lax.dynamic_slice_in_dim(slot_owner, group_index * slots_dev, slots_dev)
    slot_length = jnp.take(lengths, local_owner)
    slot_accept = jnp.take(accepted, local_owner)
    score_scale = head_size ** (-0.5)
    positions = member * cache_dev + jnp.arange(cache_dev, dtype=jnp.int32)
    visible = (positions[None, :] < slot_length[:, None])[:, None, None, :]
    cache_scores = (
        jnp.einsum("sthd,spd->sthp", queries, key_cache, preferred_element_type=jnp.float32)
        * score_scale
    )
    local_max = jnp.max(jnp.where(visible, cache_scores, -1e30), axis=-1)
    cache_probs = jnp.where(visible, jnp.exp(cache_scores - local_max[..., None]), 0.0)
    local_total = jnp.sum(cache_probs, axis=-1)
    local_out = jnp.einsum(
        "sthp,spd->sthd",
        cache_probs.astype(jnp.bfloat16),
        value_cache,
        preferred_element_type=jnp.float32,
    )
    cache_max = lax.pmax(local_max, "tok")
    factor = jnp.exp(local_max - cache_max)
    cache_total, cache_out = (
        lax.psum((local_total * factor).astype(jnp.bfloat16), "tok").astype(jnp.float32),
        lax.psum((local_out * factor[..., None]).astype(jnp.bfloat16), "tok").astype(jnp.float32),
    )
    causal = (jnp.arange(draft_len)[None, :] <= jnp.arange(draft_len)[:, None])[None, :, None, :]
    draft_scores = (
        jnp.einsum("sthd,sud->sthu", queries, keyvalue[:, :, 0], preferred_element_type=jnp.float32)
        * score_scale
    )
    draft_max = jnp.max(jnp.where(causal, draft_scores, -1e30), axis=-1)
    joint_max = jnp.maximum(cache_max, draft_max)
    cache_factor = jnp.exp(cache_max - joint_max)
    draft_probs = jnp.where(causal, jnp.exp(draft_scores - joint_max[..., None]), 0.0)
    prob_total = cache_total * cache_factor + jnp.sum(draft_probs, axis=-1)
    summed = cache_out * cache_factor[..., None] + jnp.einsum(
        "sthu,sud->sthd",
        draft_probs.astype(jnp.bfloat16),
        keyvalue[:, :, 1],
        preferred_element_type=jnp.float32,
    )
    attended = (
        (summed / prob_total[..., None])
        .astype(jnp.bfloat16)
        .reshape(group_tokens, query_heads * head_size)
    )
    attn_proj = jnp.dot(attended, attention_out, preferred_element_type=jnp.float32)
    attn_rows = lax.all_to_all(
        attn_proj.astype(jnp.bfloat16), "tok", split_axis=0, concat_axis=1, tiled=True
    ).astype(attn_proj.dtype)
    mamba_x = jnp.dot(gathered, mamba_input, preferred_element_type=jnp.float32)
    mamba_x = mamba_x.reshape(slots_dev, draft_len, heads_dev, mamba_head)
    mamba_z = jnp.dot(gathered, mamba_gate, preferred_element_type=jnp.float32)
    mamba_z = mamba_z.reshape(slots_dev, draft_len, heads_dev, mamba_head)
    both_proj = jnp.dot(gathered, state_proj, preferred_element_type=jnp.float32)
    both_proj = both_proj.reshape(slots_dev, draft_len, 2, state_size)
    step_size = jax.nn.softplus(
        jnp.dot(gathered, mamba_step, preferred_element_type=jnp.float32) + step_bias
    ).reshape(slots_dev, draft_len, heads_dev)
    decay_rate = jnp.exp(-jnp.exp(decay_log) * step_size)
    readout, chosen = recurrence(
        states,
        decay_rate,
        step_size[..., None] * mamba_x,
        both_proj[:, :, 0],
        both_proj[:, :, 1],
        slot_accept,
    )
    readout = readout + skip_gain[None, None, :, None] * mamba_x
    gated = (
        (readout * jax.nn.silu(mamba_z))
        .astype(jnp.bfloat16)
        .reshape(group_tokens, heads_dev * mamba_head)
    )
    mamba_rows = lax.psum_scatter(
        jnp.dot(gated, mamba_out, preferred_element_type=jnp.float32).astype(jnp.bfloat16),
        "tok",
        scatter_dimension=0,
        tiled=True,
    ).astype(jnp.float32)
    mixed_rows = (embedded.astype(jnp.float32) + attn_rows + mamba_rows).astype(jnp.bfloat16)
    second = rms_rows(mixed_rows, mlp_gain)
    everything = lax.all_gather(second, ("req", "tok"), axis=0, tiled=True)
    mlp_rows = lax.psum_scatter(
        feed_units(everything, gate_weight, up_weight, down_weight),
        ("req", "tok"),
        scatter_dimension=0,
        tiled=True,
    )
    hidden_out = (mixed_rows.astype(jnp.float32) + mlp_rows).astype(jnp.bfloat16)
    every_state = lax.all_gather(chosen.astype(jnp.bfloat16), "req", axis=0, tiled=True).astype(
        chosen.dtype
    )
    incoming = inverse_of(new_slot)
    local_targets = lax.dynamic_slice_in_dim(incoming, group_index * slots_dev, slots_dev)
    sources = jnp.take(current_slot, local_targets)
    new_states = jnp.take(every_state, sources, axis=0)
    return (hidden_out, new_states)


def solution(mesh):
    return jax.shard_map(
        local,
        mesh=mesh,
        in_specs=(
            P(),
            P(),
            P(),
            P(),
            P(),
            P(("req", "tok"), None),
            P(),
            P(),
            P(),
            P("req", "tok", None),
            P("req", "tok", None),
            P(None, "tok"),
            P(None, "tok"),
            P(None, "tok"),
            P(),
            P(None, "tok"),
            P("tok"),
            P("tok"),
            P("tok"),
            P("req", "tok", None, None),
            P("tok", None),
            P(),
            P(None, ("req", "tok")),
            P(None, ("req", "tok")),
            P(None, ("req", "tok")),
        ),
        out_specs=(P(("req", "tok"), None), P("req", "tok", None, None)),
        check_vma=False,
    )
```

profile of v0, /device:TPU:1, one launch (start us, length us, event | category | flops | bytes accessed | tf_op | source)
XLA Modules:
  0.0 808.4 jit_solution(15467223869452533136)
XLA Ops:
  12.4 3.9 gather_fusion.1
  16.4 6.2 convert_select_fusion
  22.5 109.7 %all-reduce.11 = bf16[512,3072]{1,0:T(8,128)(2,1)} all-reduce(f32[512,3072]{1,0:T(8,128)} %convert_select_fusion), channel_id=2, replica_groups=mesh['req'=8,'tok'=16] {'req','tok'}, use_global_device_ids=true, to_apply=%region_1.2.clone | all-reduce | flops 1572864 | bytes 9437184
  133.7 19.8 %all-gather = bf16[16,4,3072]{2,1,0:T(4,128)(2,1)} all-gather(bf16[1,4,3072]{2,1,0:T(4,128)(2,1)S(1)} %fusion.44), channel_id=1, replica_groups=mesh['req'=8,'tok'=16] {'tok'}, dimensions={0}, use_global_device_ids=true | all-gather | bytes 417792 | tf_op jit(solution)/shard_map/all_gather | solution.py:103
  154.7 3.9 convolution_convert_fusion.1
  166.3 2.9 select_reduce_fusion
  169.2 57.9 %pmax.7 = f32[4,16,6]{1,2,0:T(8,128)} all-reduce(f32[4,16,6]{1,2,0:T(8,128)S(1)} %get-tuple-element.145), channel_id=1, replica_groups=mesh['req'=8,'tok'=16] {'tok'}, use_global_device_ids=true, to_apply=%region_4.6 | all-reduce | flops 384 | bytes 3072 | tf_op jit(solution)/shard_map/pmax | solution.py:131
  234.8 3.2 fusion.54
  255.5 165.3 %while.14 = (s32[]{:T(128)}, f32[4,1,128,256]{3,2,1,0:T(8,128)}, bf16[4,1,128,256]{3,2,1,0:T(8,128)(2,1)}, f32[16,4,1,128]{3,0,1,2:T(8,128)}, f32[16,4,1]{1,2,0:...) while((s32[]{:T(128)}, f32[4,1,128,256]{3,2,1,0:T(8,128)}, ...), condition=%wide.region_12.14_spmd, body=%wide.region_10.13_spmd.sunk | while | flops 785927 | bytes 2134257 | solution.py:39
  257.6 2.6 multiply_reduce_fusion.2
  268.0 2.6 multiply_reduce_fusion.2
  288.7 2.6 multiply_reduce_fusion.2
  299.1 2.6 multiply_reduce_fusion.2
  309.4 2.6 multiply_reduce_fusion.2
  319.6 2.6 multiply_reduce_fusion.2
  330.0 2.6 multiply_reduce_fusion.2
  340.3 2.6 multiply_reduce_fusion.2
  350.6 2.6 multiply_reduce_fusion.2
  371.3 2.6 multiply_reduce_fusion.2
  428.6 2.8 fusion.5
  431.4 29.1 %psum.15 = bf16[4,16,6]{1,2,0:T(8,128)(2,1)S(1)} all-reduce(bf16[4,16,6]{1,2,0:T(8,128)(2,1)S(1)} %get-tuple-element.132), channel_id=1, replica_groups=mesh['req'=8,'tok'=16] {'tok'}, use_global_device_ids=true, to_apply=%region_8.10 | all-reduce | flops 384 | bytes 1536 | tf_op jit(solution)/shard_map/psum | solution.py:134
  462.2 68.0 %all-reduce.10.cloned.1.call-done = (bf16[4,16,6,128]{3,1,2,0:T(8,128)(2,1)}, bf16[64,3072]{1,0:T(8,128)(2,1)}) async-done(((bf16[4,16,6,128]{3,1,2,0:T(8,128)(2,1)}, bf16[64,3072]{1,0:T(8,128)(2,1)}), (bf16[4,16,6,128]{3,1,2,0:T(8,128)(2,1)}, bf16[64,3072]{1,0:T(8,128)(2,1)})) %all-reduce.10.cloned.1.call-update) | async-done | bytes 491536 | tf_op jit(solution)/shard_map/psum | solution.py:135
  532.4 3.8 all-to-all-start
  538.2 4.4 all-to-all-done
  546.1 66.2 %all-gather.7.cloned.1.call-done = bf16[128,4,3072]{2,1,0:T(4,128)(2,1)} async-done(((bf16[1,4,3072]{2,1,0:T(4,128)(2,1)}), bf16[128,4,3072]{2,1,0:T(4,128)(2,1)}) %all-gather.7.cloned.1.call-update) | async-done | bytes 3145744 | tf_op jit(solution)/shard_map/all_gather | solution.py:194
  612.3 6.0 reshape.403
  618.3 3.2 fusion.56
  621.4 6.9 fusion.7
  629.7 7.2 all-gather.5.cloned.1.call-done
  636.9 4.1 bitcast_convert_fusion
  641.0 3.6 gather_fusion.2
  646.5 153.9 %all-reduce.8.cloned.1.call-done = f32[512,3072]{1,0:T(8,128)} async-done(((f32[512,3072]{1,0:T(8,128)}), f32[512,3072]{1,0:T(8,128)}) %all-reduce.8.cloned.1.call-update) | async-done | bytes 6291472
  (221 shorter events, 189.7 us)
Async XLA Ops:
  7.2 5.3 copy-start
  7.2 523.0 %all-reduce.10.cloned.1.call-start = ((), (), s32[]{:S(2)}) async-start(), calls=%async_computation.4 | async-start | bytes 983040 | tf_op jit(solution)/shard_map/psum | solution.py:135
  22.5 110.6 %copy-start.10 = (f32[3072]{0:T(1024)S(1)}, f32[3072]{0:T(1024)}, u32[]{:S(2)}) copy-start(f32[3072]{0:T(1024)} %param.35) | copy-start | bytes 36868
  133.1 0.6 copy-start.5
  153.5 6.7 copy-start.12
  153.6 8.6 %copy-start.1 = (s32[32]{0:T(128)S(1)}, s32[32]{0:T(128)}, u32[]{:S(2)}) copy-start(s32[32]{0:T(128)} %param.30) | copy-start | bytes 388
  154.7 8.6 %copy-start.2 = (s32[32]{0:T(128)S(1)}, s32[32]{0:T(128)}, u32[]{:S(2)}) copy-start(s32[32]{0:T(128)} %param.33) | copy-start | bytes 388
  165.7 0.6 copy-start.8
  422.2 39.3 %copy-start.7 = (f32[4,16,6]{1,2,0:T(8,128)S(1)}, f32[4,16,6]{1,2,0:T(8,128)}, u32[]{:S(2)}) copy-start(f32[4,16,6]{1,2,0:T(8,128)} %pmax.7) | copy-start | bytes 4612
  422.2 108.0 %copy-start.9 = (bf16[4,16,1,128]{3,2,1,0:T(2,128)(2,1)S(1)}, bf16[4,16,1,128]{3,2,1,0:T(2,128)(2,1)}, u32[]{:S(2)}) copy-start(bf16[4,16,1,128]{3,2,1,0:T(2,128)(2,1)} %get-tuple-element.140) | copy-start | bytes 49156
  425.7 105.8 %copy-start.4 = (bf16[768,192]{0,1:T(8,128)(2,1)S(1)}, bf16[768,192]{0,1:T(8,128)(2,1)}, u32[]{:S(2)}) copy-start(bf16[768,192]{0,1:T(8,128)(2,1)} %param.40) | copy-start | bytes 884740
  427.9 114.9 %copy-start.6 = (bf16[4,3072]{1,0:T(4,128)(2,1)S(1)}, bf16[4,3072]{1,0:T(4,128)(2,1)}, u32[]{:S(2)}) copy-start(bf16[4,3072]{1,0:T(4,128)(2,1)} %copy-done.5) | copy-start | bytes 73732
  532.4 10.3 %all-to-all-start = ((bf16[16,4,192]{2,1,0:T(4,128)(2,1)}), bf16[16,4,192]{2,1,0:T(4,128)(2,1)S(1)}, u32[]{:S(2)}, u32[]{:S(2)}) async-start(bf16[16,4,192]{2,1,0:T(4,128)(2,1)} %all_to_all.10), calls=%async_computation | async-start | bytes 65536 | tf_op jit(solution)/shard_map/all_to_all | solution.py:159
  536.2 76.1 %all-gather.7.cloned.1.call-start = ((), (), s32[]{:S(2)}) async-start(), calls=%async_computation.2 | async-start | bytes 3170304 | tf_op jit(solution)/shard_map/all_gather | solution.py:194
  545.2 91.8 %all-gather.5.cloned.1.call-start = ((), (), s32[]{:S(2)}) async-start(), calls=%async_computation.1 | async-start | bytes 2359296 | tf_op jit(solution)/shard_map/all_gather | solution.py:202
  545.9 254.5 %all-reduce.8.cloned.1.call-start = ((), (), s32[]{:S(2)}) async-start(), calls=%async_computation.3 | async-start | bytes 12582912
  628.3 0.7 copy-start.11
  628.3 0.7 copy-start.3
Sparse Core Ops, SparseCore 0:
  431.5 98.6 all-reduce.9
  545.3 66.9 all-gather.6
  614.1 22.7 all-gather.4
  642.4 157.9 all-reduce.7
where the time goes:
time: 814 us; the launch traced here: 808 us
  waiting for transfers between devices  300 us (37%)
  blocking collectives  216 us (27%)
  other arithmetic  113 us (14%)
  local copies, waits for them, and re-layouts  112 us (14%)
  matrix products  35.8 us (4%)
  between operations  16.7 us (2%)
  loops' own time  9.92 us (1%)
    unnamed x5, waiting for transfers between devices  155 us
    unnamed x1, blocking collectives  110 us
    psum x1, waiting for transfers between devices, local(): lax.psum((local_out * factor[..., None]).astype(jnp.bfloat16), 'tok')  68 us
    all_gather x1, waiting for transfers between devices, local(): everything = lax.all_gather(second, ('req', 'tok'), axis=0, tiled=True)  66.2 us
    pmax x1, blocking collectives, local(): cache_max = lax.pmax(local_max, 'tok')  57.9 us
    reduce_sum x16, other arithmetic, advance(): readout = jnp.sum(current * step_read[:, None, None, :], axis=-1)  41 us
    select_n x16, other arithmetic, advance(): jnp.where((accept_count == step_index + 1)[:, None, None, None], current,...  31 us
    dynamic_slice x32, local copies, waits for them, and re-layouts, recurrence(): lax.scan(advance, (start_states, start_states), sequence)  30.9 us
  transfers between devices with their start and end apart: 5, of which 5 were waited for; matrix products, arithmetic and copies ran while one was open for 4% of the time, Pallas kernels for 0%

commit v1 on v0

--- a/solution.py
+++ b/solution.py
@@ -100,7 +100,10 @@
         tiled=True,
     ).astype(jnp.bfloat16)
     normed = rms_rows(embedded, mixer_gain)
-    gathered = lax.all_gather(normed, "tok", axis=0, tiled=True)
+    peers = lax.axis_size("tok")
+    blocks = jnp.stack([normed for _ in range(peers)])
+    blocks = lax.all_to_all(blocks, "tok", split_axis=0, concat_axis=0)
+    gathered = jnp.concatenate(blocks, axis=0)
     queries = jnp.dot(gathered, query_weight, preferred_element_type=jnp.float32).astype(
         jnp.bfloat16
     )

time: 814 us -> 629 us (0.77)
  other arithmetic: 113 us -> 25.6 us
  local copies, waits for them, and re-layouts: 112 us -> 37.2 us
  blocking collectives: 216 us -> 199 us
  matrix products: 35.8 us -> 27.4 us
    reduce_sum x16, other arithmetic: 41 us -> 5.23 us  [advance(): readout = jnp.sum(current * step_read[:, None, None, :], axis=-1)]
    select_n x16, other arithmetic: 31 us -> 2 us  [advance(): jnp.where((accept_count == step_index + 1)[:, None, None, None], current,...]
    dynamic_slice x32 -> x80, local copies, waits for them, and re-layouts: 30.9 us -> 9.99 us  [recurrence(): lax.scan(advance, (start_states, start_states), sequence)]
    dynamic_update_slice x16, local copies, waits for them, and re-layouts: 21.3 us -> 0.6 us  [recurrence(): lax.scan(advance, (start_states, start_states), sequence)]
    all_gather x1 -> x0, blocking collectives: 19.8 us -> none  [local(): gathered = lax.all_gather(normed, 'tok', axis=0, tiled=True)]
    mul x16 -> x0, local copies, waits for them, and re-layouts: 11 us -> none  [advance(): readout = jnp.sum(current * step_read[:, None, None, :], axis=-1)]
    mul x16, local copies, waits for them, and re-layouts: 10.3 us -> 0.15 us  [advance(): step_decay[:, :, None, None] * current]
    eq x16, other arithmetic: 10 us -> 0.1 us  [advance(): accept_count == step_index + 1]
  transfers between devices with their start and end apart: 5 -> 6, of which waited for: 5 -> 6; matrix products, arithmetic and copies ran while one was open for 4% -> 5% of each run, Pallas kernels for 0% -> 0%
where the time goes in v1:
time: 629 us; the launch traced here: 627 us
  waiting for transfers between devices  301 us (48%)
  blocking collectives  199 us (32%)
  local copies, waits for them, and re-layouts  37.2 us (6%)
  matrix products  27.4 us (4%)
  other arithmetic  25.6 us (4%)
  between operations  16.8 us (3%)
  loops' own time  11.5 us (2%)
  starting transfers between devices  9.23 us (1%)
    unnamed x5, waiting for transfers between devices  155 us
    unnamed x1, blocking collectives  110 us
    all_gather x1, waiting for transfers between devices, local(): everything = lax.all_gather(second, ('req', 'tok'), axis=0, tiled=True)  66.3 us
    psum x1, waiting for transfers between devices, local(): lax.psum((local_out * factor[..., None]).astype(jnp.bfloat16), 'tok')  63.4 us
    pmax x1, blocking collectives, local(): cache_max = lax.pmax(local_max, 'tok')  59.9 us
    psum x1, blocking collectives, local(): lax.psum((local_total * factor).astype(jnp.bfloat16), 'tok')  29.1 us
  transfers between devices with their start and end apart: 6, of which 6 were waited for; matrix products, arithmetic and copies ran while one was open for 5% of the time, Pallas kernels for 0%

profile of v1, /device:TPU:1, one launch (start us, length us, event | category | flops | bytes accessed | tf_op | source)
XLA Modules:
  0.0 627.3 jit_solution(11211211360543480838)
XLA Ops:
  7.2 2.0 copy.154
  11.8 3.9 gather_fusion.1
  15.7 6.2 convert_select_fusion
  21.9 109.7 %all-reduce.11 = bf16[512,3072]{1,0:T(8,128)(2,1)} all-reduce(f32[512,3072]{1,0:T(8,128)} %convert_select_fusion), channel_id=2, replica_groups=mesh['req'=8,'tok'=16] {'req','tok'}, use_global_device_ids=true, to_apply=%region_1.2.clone | all-reduce | flops 1572864 | bytes 9437184
  133.5 5.1 all-to-all-start
  141.5 4.7 copy.93
  147.8 3.3 convolution_convert_fusion.1
  151.2 1.8 select_reduce_fusion
  153.0 59.9 %pmax.7 = f32[4,16,6]{1,2,0:T(8,128)S(1)} all-reduce(f32[4,16,6]{1,2,0:T(8,128)S(1)} %get-tuple-element.145), channel_id=1, replica_groups=mesh['req'=8,'tok'=16] {'tok'}, use_global_device_ids=true, to_apply=%region_4.6 | all-reduce | flops 384 | bytes 3072 | tf_op jit(solution)/shard_map/pmax | solution.py:134
  213.3 1.8 convolution_convert_fusion.2
  215.2 1.4 fusion.53
  218.0 3.1 fusion.16
  221.2 29.6 %while.14 = (s32[]{:T(128)}, f32[4,1,128,256]{3,2,1,0:T(8,128)S(1)}, bf16[4,1,128,256]{3,2,1,0:T(8,128)(2,1)S(1)}, f32[16,4,1,128]{3,0,1,2:T(8,128)S(1)}, f32[16...) while((s32[]{:T(128)}, ...), condition=%wide.region_12.14_spmd, body=%wide.region_10.13_spmd.sunk | while | flops 785927 | bytes 2150641 | solution.py:39
  250.7 1.5 fusion.54
  252.6 2.2 convolution_convert_fusion
  254.9 2.3 fusion.5
  257.2 29.1 %psum.15 = bf16[4,16,6]{1,2,0:T(8,128)(2,1)S(1)} all-reduce(bf16[4,16,6]{1,2,0:T(8,128)(2,1)S(1)} %get-tuple-element.132), channel_id=1, replica_groups=mesh['req'=8,'tok'=16] {'tok'}, use_global_device_ids=true, to_apply=%region_8.10 | all-reduce | flops 384 | bytes 1536 | tf_op jit(solution)/shard_map/psum | solution.py:137
  286.4 63.4 %all-reduce.10.cloned.1.call-done = (bf16[4,16,6,128]{3,1,2,0:T(8,128)(2,1)}, bf16[64,3072]{1,0:T(8,128)(2,1)}) async-done(((bf16[4,16,6,128]{3,1,2,0:T(8,128)(2,1)}, bf16[64,3072]{1,0:T(8,128)(2,1)}), (bf16[4,16,6,128]{3,1,2,0:T(8,128)(2,1)}, bf16[64,3072]{1,0:T(8,128)(2,1)})) %all-reduce.10.cloned.1.call-update) | async-done | bytes 491536 | tf_op jit(solution)/shard_map/psum | solution.py:138
  349.8 1.1 fusion.4
  351.9 3.8 all-to-all-start.1
  357.2 5.0 all-to-all-done.1
  362.3 1.0 fusion.39
  364.8 66.3 %all-gather.6.cloned.1.call-done = bf16[128,4,3072]{2,1,0:T(4,128)(2,1)} async-done(((bf16[1,4,3072]{2,1,0:T(4,128)(2,1)}), bf16[128,4,3072]{2,1,0:T(4,128)(2,1)}) %all-gather.6.cloned.1.call-update) | async-done | bytes 3145744 | tf_op jit(solution)/shard_map/all_gather | solution.py:197
  431.1 4.5 reshape.407
  435.6 2.2 fusion.55
  437.8 6.0 fusion.7
  445.1 10.7 %all-gather.4.cloned.1.call-done = bf16[32,1,128,256]{3,2,1,0:T(8,128)(2,1)} async-done(((bf16[4,1,128,256]{3,2,1,0:T(8,128)(2,1)}), bf16[32,1,128,256]{3,2,1,0:T(8,128)(2,1)}) %all-gather.4.cloned.1.call-update) | async-done | bytes 2097168 | tf_op jit(solution)/shard_map/all_gather | solution.py:205
  455.8 4.0 bitcast_convert_fusion
  459.9 3.6 gather_fusion.2
  463.4 1.9 fusion.15
  465.4 153.9 %all-reduce.8.cloned.1.call-done = f32[512,3072]{1,0:T(8,128)} async-done(((f32[512,3072]{1,0:T(8,128)}), f32[512,3072]{1,0:T(8,128)}) %all-reduce.8.cloned.1.call-update) | async-done | bytes 6291472
  619.3 1.5 fusion.42
  (255 shorter events, 32.1 us)
Async XLA Ops:
  7.2 4.6 copy-start
  21.9 110.7 %copy-start.8 = (f32[3072]{0:T(1024)S(1)}, f32[3072]{0:T(1024)}, u32[]{:S(2)}) copy-start(f32[3072]{0:T(1024)} %param.35) | copy-start | bytes 36868
  21.9 116.8 %copy-start.11 = (s32[32]{0:T(128)S(1)}, s32[32]{0:T(128)}, u32[]{:S(2)}) copy-start(s32[32]{0:T(128)} %param.32) | copy-start | bytes 388
  21.9 117.0 %copy-start.2 = (s32[32]{0:T(128)S(1)}, s32[32]{0:T(128)}, u32[]{:S(2)}) copy-start(s32[32]{0:T(128)} %param.30) | copy-start | bytes 388
  21.9 117.6 %copy-start.3 = (s32[32]{0:T(128)S(1)}, s32[32]{0:T(128)}, u32[]{:S(2)}) copy-start(s32[32]{0:T(128)} %param.33) | copy-start | bytes 388
  133.5 14.2 %all-to-all-start = ((bf16[16,4,3072]{2,1,0:T(4,128)(2,1)}), bf16[16,4,3072]{2,1,0:T(4,128)(2,1)S(1)}, u32[]{:S(2)}, u32[]{:S(2)}) async-start(bf16[16,4,3072]{2,1,0:T(4,128)(2,1)} %stack.2), calls=%async_computation | async-start | bytes 786432 | tf_op jit(solution)/shard_map/all_to_all | solution.py:105
  138.6 211.2 %all-reduce.10.cloned.1.call-start = ((), (), s32[]{:S(2)}) async-start(), calls=%async_computation.5 | async-start | bytes 983040 | tf_op jit(solution)/shard_map/psum | solution.py:138
  141.5 4.7 copy-start.5
  153.0 63.6 %copy-start.10 = (bf16[3072,1]{0,1:T(2,128)(2,1)S(1)}, bf16[3072,1]{0,1:T(2,128)(2,1)}, u32[]{:S(2)}) copy-start(bf16[3072,1]{0,1:T(2,128)(2,1)} %param.44) | copy-start | bytes 18436
  250.7 6.5 %copy-start.6 = (bf16[4,1,128,256]{3,2,1,0:T(8,128)(2,1)}, bf16[4,1,128,256]{3,2,1,0:T(8,128)(2,1)S(1)}, u32[]{:S(2)}) copy-start(bf16[4,1,128,256]{3,2,1,0:T(8,128)(2,1)S(1)} %get-tuple-element.57) | copy-start | bytes 786436
  252.6 98.4 %copy-start.7 = (bf16[768,192]{0,1:T(8,128)(2,1)S(1)}, bf16[768,192]{0,1:T(8,128)(2,1)}, u32[]{:S(2)}) copy-start(bf16[768,192]{0,1:T(8,128)(2,1)} %param.40) | copy-start | bytes 884740
  254.8 101.1 %copy-start.12 = (u32[128]{0:T(128)S(1)}, u32[128]{0:T(128)}, u32[]{:S(2)}) copy-start(u32[128]{0:T(128)} %constant.131) | copy-start | bytes 1540
  254.9 108.4 %copy-start.9 = (f32[3072]{0:T(1024)S(1)}, f32[3072]{0:T(1024)}, u32[]{:S(2)}) copy-start(f32[3072]{0:T(1024)} %param.50) | copy-start | bytes 36868
  351.9 10.3 %all-to-all-start.1 = ((bf16[16,4,192]{2,1,0:T(4,128)(2,1)}), bf16[16,4,192]{2,1,0:T(4,128)(2,1)S(1)}, u32[]{:S(2)}, u32[]{:S(2)}) async-start(bf16[16,4,192]{2,1,0:T(4,128)(2,1)} %all_to_all.14), calls=%async_computation.1 | async-start | bytes 65536 | tf_op jit(solution)/shard_map/all_to_all | solution.py:162
  355.7 75.4 %all-gather.6.cloned.1.call-start = ((), (), s32[]{:S(2)}) async-start(), calls=%async_computation.3 | async-start | bytes 3170304 | tf_op jit(solution)/shard_map/all_gather | solution.py:197
  364.0 91.9 %all-gather.4.cloned.1.call-start = ((), (), s32[]{:S(2)}) async-start(), calls=%async_computation.2 | async-start | bytes 2359296 | tf_op jit(solution)/shard_map/all_gather | solution.py:205
  364.7 254.6 %all-reduce.8.cloned.1.call-start = ((), (), s32[]{:S(2)}) async-start(), calls=%async_computation.4 | async-start | bytes 12582912
  443.8 0.7 copy-start.4
  445.1 175.7 %copy-start.1 = (bf16[512,3072]{1,0:T(8,128)(2,1)S(1)}, bf16[512,3072]{1,0:T(8,128)(2,1)}, u32[]{:S(2)}) copy-start(bf16[512,3072]{1,0:T(8,128)(2,1)} %param.34) | copy-start | bytes 9437188
Sparse Core Ops, SparseCore 0:
  257.3 92.4 all-reduce.9
  364.1 66.9 all-gather.5
  432.9 22.8 all-gather.3
  461.3 157.9 all-reduce.7
